TPU v7x, 512 devices: a whole 4x8x8 slice. The times are simulated.
512 devices in a mesh: node: 128 (over z, y, core), feat: 4 (over x).
Axes of the slice: x: 4, y: 8, z: 8, core: 2. Of those that a mesh axis runs over, the one named last changes fastest.
Arguments:
- embed: bfloat16 [256, 131072], P('feat', 'node'), may hold values from -6 to 6
- tile_weight: bfloat16 [128, 135, 128, 128], P('node'), may hold values from -0.125 to 0.125
- tile_rows: int32 [128, 135], P('node'), may hold values from 0 to 7
- tile_cols: int32 [128, 135], P('node'), may hold values from 0 to 135, as said below
- send_rows: int32 [128, 128], P('node'), may hold values from 0 to 7
- src_local: int32 [65536], P('node'), may hold values from 0 to 1023
- dst_owner: int32 [65536, 1], P('node'), may hold values from 0 to 127; in each aligned block of 512 rows (0 to 511, 512 to 1023, ...) at most 8 rows name the same one
- dst_local: int32 [65536], P('node'), may hold values from 0 to 1023
- w_in: bfloat16 [256, 1024], P('feat'), may hold values from -0.375 to 0.375
- b_in: float32 [1024], replicated, may hold values from -4 to 4
- w_out: float32 [1024], replicated, may hold values from -0.1875 to 0.1875
Outputs:
- propagated: bfloat16 [256, 131072], P('feat', 'node')
- scores: float32 [65536], P('node')
Inputs may be any that keep to these rules, and one draw needn't show every extreme that they name: In each part, the entries of tile_cols below 8 are the numbers 0 to 7 once each, and tile_rows equals tile_cols at those tiles; the other 127 entries are 8 + p for every part p other than the part itself, once each. `dst_owner`: among the 512 queries of one part, at most 8 have the same destination part, and exactly 8 do for some destination part.
All inputs are finite; a program needn't handle non-finite values.
Results may differ from a plain program's by a relative error of at most 0.015.
Values may be sent and summed in bfloat16 or wider, within the bound.
A program may use at most 64 MiB of HBM per device.

v0:
```python
import jax
import jax.numpy as jnp
from jax import lax
from jax.sharding import PartitionSpec as P

HOPS = 2
TELEPORT = 0.1


def propagate(current, initial, weights, tile_row, tile_col, targets):
    channels, node_count = current.shape
    block_size = weights.shape[-1]
    block_count = node_count // block_size
    blocked = current.reshape(channels, block_count, block_size)
    outgoing = blocked[:, targets, :]
    incoming = lax.all_to_all(outgoing, "node", split_axis=1, concat_axis=1, tiled=True)
    sources = jnp.concatenate([blocked, incoming], axis=1)
    picked = sources[:, tile_col, :]
    products = jnp.einsum("ctj,tij->cti", picked, weights, preferred_element_type=jnp.float32)
    selector = (tile_row[None, :] == jnp.arange(block_count, dtype=jnp.int32)[:, None]).astype(
        jnp.float32
    )
    summed = jnp.einsum("rt,cti->cri", selector, products, precision=lax.Precision.HIGHEST)
    return ((1.0 - TELEPORT) * summed.reshape(channels, node_count) + TELEPORT * initial).astype(
        jnp.bfloat16
    )


def contract_rows(left_matrix, right_matrix):
    return lax.dot_general(
        left_matrix, right_matrix, (((0,), (0,)), ((), ())), preferred_element_type=jnp.float32
    )


def shards(
    embed,
    tile_weight,
    tile_rows,
    tile_cols,
    send_rows,
    src_local,
    dst_owner,
    dst_local,
    w_in,
    b_in,
    w_out,
):
    weights = tile_weight[0]
    tile_row = tile_rows[0]
    tile_col = tile_cols[0]
    targets = send_rows[0]
    initial = embed.astype(jnp.float32)
    current = embed
    for hop_index in range(HOPS):
        current = propagate(current, initial, weights, tile_row, tile_col, targets)
    part_count = lax.axis_size("node")
    queries = src_local.shape[0]
    capacity = max(2, 2 * queries // part_count)
    owners = dst_owner[:, 0]
    owner_hits = (owners[:, None] == jnp.arange(part_count, dtype=jnp.int32)[None, :]).astype(
        jnp.int32
    )
    slot_rank = jnp.sum(jnp.cumsum(owner_hits, axis=0) * owner_hits, axis=1) - 1
    requests = (
        jnp.zeros((part_count * capacity,), jnp.int32)
        .at[owners * capacity + slot_rank]
        .set(dst_local)
    )
    requests = requests.reshape(part_count, capacity)
    replies = lax.all_to_all(
        current[:, lax.all_to_all(requests, "node", split_axis=0, concat_axis=0, tiled=True)],
        "node",
        split_axis=1,
        concat_axis=1,
        tiled=True,
    )
    target_rows = replies[:, owners, slot_rank]
    source_rows = current[:, src_local]
    hadamard = (source_rows.astype(jnp.float32) * target_rows.astype(jnp.float32)).astype(
        jnp.bfloat16
    )
    partial_value = contract_rows(w_in, hadamard)
    hidden = lax.psum(partial_value.astype(jnp.bfloat16), "feat").astype(jnp.float32)
    active = jnp.maximum(hidden + b_in[:, None], 0.0)
    scores = jnp.dot(w_out, active, precision=lax.Precision.HIGHEST)
    return (current, scores)


def solution(mesh):
    placed = (
        P("feat", "node"),
        P("node", None, None, None),
        P("node", None),
        P("node", None),
        P("node", None),
        P("node"),
        P("node", None),
        P("node"),
        P("feat", None),
        P(),
        P(),
    )
    return jax.shard_map(
        shards,
        mesh=mesh,
        in_specs=placed,
        out_specs=(P("feat", "node"), P("node")),
        check_vma=False,
    )
```

profile of v0, /device:TPU:8, one launch (start us, length us, event | category | flops | bytes accessed | tf_op | source)
XLA Modules:
  0.0 273.8 jit_solution(4774526276266268185)
XLA Ops:
  7.2 0.0 copy-start
  7.2 1.0 copy_bitcast_fusion
  8.1 0.7 fusion.56
  8.8 2.2 gather_fusion
  11.0 0.0 copy-start.1
  11.0 0.0 copy-start.2
  11.0 0.0 copy-start.5
  11.0 17.5 %all-to-all-start = ((bf16[64,128,128]{2,0,1:T(8,128)(2,1)}), bf16[64,128,128]{2,0,1:T(8,128)(2,1)S(1)}, u32[]{:S(2)}, u32[]{:S(2)}) async-start(bf16[64,128,128]{2,0,1:T(8,128)(2,1)} %bitcast.90), calls=%async_computation | async-start | bytes 4194304 | tf_op jit(solution)/shard_map/all_to_all | solution.py:16
  28.5 0.0 copy-done.1
  28.5 0.2 copy.72
  28.7 0.0 copy-done.2
  28.7 0.1 copy.79
  28.8 0.2 fusion.42
  29.1 0.2 fusion.41
  29.4 2.6 scatter_custom_fusion
  32.0 0.7 all_to_all.19
  32.7 0.0 copy-done.5
  32.7 49.8 %all-to-all-done = bf16[64,128,128]{2,0,1:T(8,128)(2,1)S(1)} async-done(((bf16[64,128,128]{2,0,1:T(8,128)(2,1)}), bf16[64,128,128]{2,0,1:T(8,128)(2,1)S(1)}, u32[]{:S(2)}, u32[]{:S(2)}) %all-to-all-start) | async-done | bytes 2097184 | tf_op jit(solution)/shard_map/all_to_all | solution.py:16
  82.5 6.1 %all-to-all-start.2 = ((s32[128,1,8]{2,1,0:T(1,128)}), s32[128,1,8]{2,1,0:T(1,128)S(1)}, u32[]{:S(2)}, u32[]{:S(2)}) async-start(s32[128,1,8]{2,1,0:T(1,128)} %bitcast.25), calls=%async_computation.2 | async-start | bytes 131072 | tf_op jit(solution)/shard_map/all_to_all | solution.py:71
  88.6 1.6 pad_maximum_fusion
  90.2 2.6 gather_fusion.1
  92.8 0.0 copy-start.3
  92.8 5.4 %fusion.10 = f32[64,135,128]{2,0,1:T(8,128)S(1)} fusion(bf16[1,135,128,128]{3,2,1,0:T(8,128)(2,1)} %param.12, bf16[135,64,128]{2,1,0:T(8,128)(2,1)S(1)} %gather_fusion.1), kind=kOutput, calls=%fused_computation.20 | convolution fusion | flops 283115520 | bytes 11059200 | tf_op jit(solution)/shard_map/ctj,tij->cti/dot_general | solution.py:19
  98.2 0.0 copy-done.3
  98.2 4.0 %fusion.34 = f32[64,8,128]{2,1,0:T(8,128)S(1)} fusion(f32[64,135,128]{2,0,1:T(8,128)S(1)} %fusion.10, s32[135]{0:T(256)S(1)} %bitcast.101), kind=kOutput, calls=%fused_computation.31 | convolution fusion | flops 106234936 | bytes 4686364 | tf_op jit(solution)/shard_map/rt,cti->cri/dot_general | solution.py:23
  102.2 0.2 copy.83
  102.5 0.1 fusion.40
  102.5 0.1 copy.76
  102.7 2.2 gather_fusion.2
  104.8 0.0 all-to-all-done.2
  104.8 13.7 %all-to-all-start.1 = ((bf16[64,128,128]{2,0,1:T(8,128)(2,1)}), bf16[64,128,128]{2,0,1:T(8,128)(2,1)S(1)}, u32[]{:S(2)}, u32[]{:S(2)}) async-start(bf16[64,128,128]{2,0,1:T(8,128)(2,1)} %bitcast.13), calls=%async_computation.1 | async-start | bytes 4194304 | tf_op jit(solution)/shard_map/all_to_all | solution.py:16
  118.6 0.1 reshape.190
  118.7 53.9 %all-to-all-done.1 = bf16[64,128,128]{2,0,1:T(8,128)(2,1)S(1)} async-done(((bf16[64,128,128]{2,0,1:T(8,128)(2,1)}), bf16[64,128,128]{2,0,1:T(8,128)(2,1)S(1)}, u32[]{:S(2)}, u32[]{:S(2)}) %all-to-all-start.1) | async-done | bytes 2097184 | tf_op jit(solution)/shard_map/all_to_all | solution.py:16
  172.6 1.6 pad_maximum_fusion.1
  174.2 2.6 gather_fusion.3
  176.8 5.4 %fusion.15 = f32[64,135,128]{2,0,1:T(8,128)S(1)} fusion(bf16[1,135,128,128]{3,2,1,0:T(8,128)(2,1)} %param.12, bf16[135,64,128]{2,1,0:T(8,128)(2,1)S(1)} %gather_fusion.3), kind=kOutput, calls=%fused_computation.21 | convolution fusion | flops 283115520 | bytes 11059200 | tf_op jit(solution)/shard_map/ctj,tij->cti/dot_general | solution.py:19
  182.2 4.0 %fusion.31 = f32[64,8,128]{2,1,0:T(8,128)S(1)} fusion(f32[64,135,128]{2,0,1:T(8,128)S(1)} %fusion.15, s32[135]{0:T(256)S(1)} %bitcast.102), kind=kOutput, calls=%fused_computation.30 | convolution fusion | flops 106234936 | bytes 4686364 | tf_op jit(solution)/shard_map/rt,cti->cri/dot_general | solution.py:23
  186.2 0.2 copy.87
  186.4 0.1 fusion.39
  186.5 0.0 copy-start.4
  186.5 3.2 %gather_fusion.5 = bf16[1024,64]{1,0:T(8,128)(2,1)S(1)} fusion(bf16[64,1024]{0,1:T(8,128)(2,1)S(1)} %fusion.39, s32[1024]{0:T(1024)S(1)} %broadcast_clamp_fusion), kind=kCustom, calls=%fused_computation.5 | custom fusion | bytes 266240 | tf_op jit(solution)/shard_map/gather | solution.py:71
  189.8 0.9 reshape.217
  190.7 6.2 %all-to-all-start.3 = ((bf16[128,2,256]{2,1,0:T(2,128)(2,1)}), bf16[128,2,256]{2,1,0:T(2,128)(2,1)S(1)}, u32[]{:S(2)}, u32[]{:S(2)}) async-start(bf16[128,2,256]{2,1,0:T(2,128)(2,1)} %reshape.217), calls=%async_computation.3 | async-start | bytes 262144 | tf_op jit(solution)/shard_map/all_to_all | solution.py:70
  196.8 0.3 all-reduce.2.cloned.1.call-start
  197.1 0.0 copy-done.4
  197.2 1.3 gather_fusion.4
  198.5 0.0 copy-start.6
  198.5 0.0 copy-start.7
  198.6 10.2 %all-to-all-done.3 = bf16[128,2,256]{2,1,0:T(2,128)(2,1)S(1)} async-done(((bf16[128,2,256]{2,1,0:T(2,128)(2,1)}), bf16[128,2,256]{2,1,0:T(2,128)(2,1)S(1)}, u32[]{:S(2)}, u32[]{:S(2)}) %all-to-all-start.3) | async-done | bytes 131104 | tf_op jit(solution)/shard_map/all_to_all | solution.py:70
  208.8 0.2 reshape.218
  209.0 3.1 %gather_fusion.6 = bf16[512,64]{1,0:T(8,128)(2,1)S(1)} fusion(bf16[64,128,8]{0,2,1:T(8,128)(2,1)S(1)} %bitcast.91, s32[512]{0:T(512)S(1)} %bitcast.89), kind=kCustom, calls=%fused_computation.6 | custom fusion | bytes 135168 | tf_op jit(solution)/shard_map/gather | solution.py:77
  212.1 0.0 copy-done
  212.1 1.5 fusion.24
  213.5 0.0 all-reduce.2.cloned.1.call-update
  213.6 0.8 copy.82
  214.4 48.7 %all-reduce.2.cloned.1.call-done = bf16[1024,512]{0,1:T(8,128)(2,1)} async-done(((bf16[1024,512]{0,1:T(8,128)(2,1)}), bf16[1024,512]{0,1:T(8,128)(2,1)}) %all-reduce.2.cloned.1.call-update) | async-done | bytes 1048592 | tf_op jit(solution)/shard_map/psum | solution.py:83
  263.1 0.0 copy-done.6
  263.1 0.0 copy-done.7
  263.1 3.9 %fusion.20 = f32[1,512]{1,0:T(1,128)} fusion(f32[1024,1]{0,1:T(1,128)S(1)} %bitcast.105, bf16[1024,512]{0,1:T(8,128)(2,1)} %all-reduce.2.cloned.1.call-done, f32[1024]{0:T(1024)S(1)} %copy-done.7), kind=kOutput, calls=%fused_computation.22 | convolution fusion | flops 7864320 | bytes 1058816 | tf_op jit(solution)/shard_map/dot_general | solution.py:85
  (16 shorter events, 0.2 us)
Async XLA Ops:
  7.2 204.9 %copy-start = (bf16[64,1024]{1,0:T(8,128)(2,1)S(1)}, bf16[64,1024]{1,0:T(8,128)(2,1)}, u32[]{:S(2)}) copy-start(bf16[64,1024]{1,0:T(8,128)(2,1)} %param.19) | copy-start | bytes 393220
  11.0 17.5 %copy-start.1 = (bf16[64,1024]{1,0:T(8,128)(2,1)S(1)}, bf16[64,1024]{1,0:T(8,128)(2,1)}, u32[]{:S(2)}) copy-start(bf16[64,1024]{1,0:T(8,128)(2,1)} %param.11) | copy-start | bytes 393220
  11.0 17.7 %copy-start.2 = (s32[512,1]{0,1:T(1,128)S(1)}, s32[512,1]{0,1:T(1,128)}, u32[]{:S(2)}) copy-start(s32[512,1]{0,1:T(1,128)} %param.17) | copy-start | bytes 6148
  11.0 21.7 %copy-start.5 = (s32[1,135]{1,0:T(1,128)S(1)}, s32[1,135]{1,0:T(1,128)}, u32[]{:S(2)}) copy-start(s32[1,135]{1,0:T(1,128)} %param.14) | copy-start | bytes 1624
  11.0 71.6 %all-to-all-start = ((bf16[64,128,128]{2,0,1:T(8,128)(2,1)}), bf16[64,128,128]{2,0,1:T(8,128)(2,1)S(1)}, u32[]{:S(2)}, u32[]{:S(2)}) async-start(bf16[64,128,128]{2,0,1:T(8,128)(2,1)} %bitcast.90), calls=%async_computation | async-start | bytes 4194304 | tf_op jit(solution)/shard_map/all_to_all | solution.py:16
  82.5 22.3 %all-to-all-start.2 = ((s32[128,1,8]{2,1,0:T(1,128)}), s32[128,1,8]{2,1,0:T(1,128)S(1)}, u32[]{:S(2)}, u32[]{:S(2)}) async-start(s32[128,1,8]{2,1,0:T(1,128)} %bitcast.25), calls=%async_computation.2 | async-start | bytes 131072 | tf_op jit(solution)/shard_map/all_to_all | solution.py:71
  92.8 5.4 %copy-start.3 = (s32[1,135]{1,0:T(1,128)S(1)}, s32[1,135]{1,0:T(1,128)}, u32[]{:S(2)}) copy-start(s32[1,135]{1,0:T(1,128)} %param.13) | copy-start | bytes 1624
  104.8 67.8 %all-to-all-start.1 = ((bf16[64,128,128]{2,0,1:T(8,128)(2,1)}), bf16[64,128,128]{2,0,1:T(8,128)(2,1)S(1)}, u32[]{:S(2)}, u32[]{:S(2)}) async-start(bf16[64,128,128]{2,0,1:T(8,128)(2,1)} %bitcast.13), calls=%async_computation.1 | async-start | bytes 4194304 | tf_op jit(solution)/shard_map/all_to_all | solution.py:16
  186.5 10.6 %copy-start.4 = (s32[512]{0:T(512)S(1)}, s32[512]{0:T(512)}, u32[]{:S(2)}) copy-start(s32[512]{0:T(512)} %param.16) | copy-start | bytes 6148
  190.7 18.1 %all-to-all-start.3 = ((bf16[128,2,256]{2,1,0:T(2,128)(2,1)}), bf16[128,2,256]{2,1,0:T(2,128)(2,1)S(1)}, u32[]{:S(2)}, u32[]{:S(2)}) async-start(bf16[128,2,256]{2,1,0:T(2,128)(2,1)} %reshape.217), calls=%async_computation.3 | async-start | bytes 262144 | tf_op jit(solution)/shard_map/all_to_all | solution.py:70
  196.8 66.2 %all-reduce.2.cloned.1.call-start = ((), (), s32[]{:S(2)}) async-start(), calls=%async_computation.4 | async-start | bytes 2097152 | tf_op jit(solution)/shard_map/psum | solution.py:83
  198.5 64.6 %copy-start.6 = (f32[1024]{0:T(1024)S(1)}, f32[1024]{0:T(1024)}, u32[]{:S(2)}) copy-start(f32[1024]{0:T(1024)} %param.21) | copy-start | bytes 12292
  198.5 64.5 %copy-start.7 = (f32[1024]{0:T(1024)S(1)}, f32[1024]{0:T(1024)}, u32[]{:S(2)}) copy-start(f32[1024]{0:T(1024)} %param.20) | copy-start | bytes 12292
Sparse Core Ops, SparseCore 0:
  213.7 49.3 all-reduce.1
where the time goes:
time: 274 us
  waiting for transfers between devices  163 us (59%)
  starting transfers between devices  43.8 us (16%)
  local copies, waits for them, and re-layouts  24.4 us (9%)
  matrix products  24.1 us (9%)
  between operations  14.3 us (5%)
  other arithmetic  4.5 us (2%)
    all_to_all x2, waiting for transfers between devices, propagate(): lax.all_to_all(outgoing, 'node', split_axis=1, concat_axis=1, tiled=True)  104 us
    psum x1, waiting for transfers between devices, shards(): lax.psum(partial_value.astype(jnp.bfloat16), 'feat').astype(jnp.float32)  48.7 us
    all_to_all x2, starting transfers between devices, propagate(): lax.all_to_all(outgoing, 'node', split_axis=1, concat_axis=1, tiled=True)  31.2 us
    dot_general x2, matrix products, propagate(): jnp.einsum('ctj,tij->cti', picked, weights, preferred_element_type=jnp.fl...  10.8 us
    all_to_all x1, waiting for transfers between devices, shards(): lax.all_to_all(current[:, lax.all_to_all(requests, 'node', split_axis=0,...  10.2 us
    dot_general x2, matrix products, propagate(): jnp.einsum('rt,cti->cri', selector, products, precision=lax.Precision.HIG...  7.96 us
    all_to_all x1, starting transfers between devices, shards(): lax.all_to_all(current[:, lax.all_to_all(requests, 'node', split_axis=0,...  6.16 us
    all_to_all x1, starting transfers between devices, shards(): lax.all_to_all(requests, 'node', split_axis=0, concat_axis=0, tiled=True)  6.07 us
  transfers between devices with their start and end apart: 5, of which 4 were waited for; matrix products, arithmetic and copies ran while one was open for 8% of the time, Pallas kernels for 0%

commit v1 on v0

--- a/solution.py
+++ b/solution.py
@@ -67,12 +67,22 @@
         .set(dst_local)
     )
     requests = requests.reshape(part_count, capacity)
-    replies = lax.all_to_all(
-        current[:, lax.all_to_all(requests, "node", split_axis=0, concat_axis=0, tiled=True)],
-        "node",
-        split_axis=1,
-        concat_axis=1,
-        tiled=True,
+    replies = jnp.concatenate(
+        lax.all_to_all(
+            jnp.stack(
+                jnp.split(
+                    current[
+                        :, lax.all_to_all(requests, "node", split_axis=0, concat_axis=0, tiled=True)
+                    ],
+                    lax.axis_size("node"),
+                    axis=1,
+                )
+            ),
+            "node",
+            0,
+            0,
+        ),
+        axis=1,
     )
     target_rows = replies[:, owners, slot_rank]
     source_rows = current[:, src_local]

time: 274 us -> 277 us (1.011)
  no operation moved by 1% of the time
where the time goes in v1:
time: 277 us; the launch traced here: 276 us
  waiting for transfers between devices  163 us (59%)
  starting transfers between devices  43.8 us (16%)
  local copies, waits for them, and re-layouts  25.4 us (9%)
  matrix products  24.1 us (9%)
  between operations  14.7 us (5%)
  other arithmetic  5.21 us (2%)
    all_to_all x2, waiting for transfers between devices, propagate(): lax.all_to_all(outgoing, 'node', split_axis=1, concat_axis=1, tiled=True)  104 us
    psum x1, waiting for transfers between devices, shards(): lax.psum(partial_value.astype(jnp.bfloat16), 'feat').astype(jnp.float32)  48.7 us
    all_to_all x2, starting transfers between devices, propagate(): lax.all_to_all(outgoing, 'node', split_axis=1, concat_axis=1, tiled=True)  31.2 us
    dot_general x2, matrix products, propagate(): jnp.einsum('ctj,tij->cti', picked, weights, preferred_element_type=jnp.fl...  10.8 us
    all_to_all x1, waiting for transfers between devices, shards(): lax.all_to_all(jnp.stack(jnp.split(current[:, lax.all_to_all(requests, 'n...  10.3 us
    dot_general x2, matrix products, propagate(): jnp.einsum('rt,cti->cri', selector, products, precision=lax.Precision.HIG...  7.96 us
    all_to_all x1, starting transfers between devices, shards(): lax.all_to_all(jnp.stack(jnp.split(current[:, lax.all_to_all(requests, 'n...  6.16 us
    all_to_all x1, starting transfers between devices, shards(): lax.all_to_all(requests, 'node', split_axis=0, concat_axis=0, tiled=True)  6.07 us
  transfers between devices with their start and end apart: 5, of which 4 were waited for; matrix products, arithmetic and copies ran while one was open for 8% of the time, Pallas kernels for 0%

profile of v1, /device:TPU:8, one launch (start us, length us, event | category | flops | bytes accessed | tf_op | source)
XLA Modules:
  0.0 276.0 jit_solution(10958176911067411110)
XLA Ops:
  7.2 0.0 copy-start
  7.2 0.7 compare_select_fusion.5
  7.9 0.7 fusion.56
  8.6 0.9 copy_bitcast_fusion
  9.5 2.2 gather_fusion
  11.7 0.0 copy-start.1
  11.7 0.0 copy-start.2
  11.7 0.0 copy-start.4
  11.7 17.5 %all-to-all-start = ((bf16[64,128,128]{2,0,1:T(8,128)(2,1)}), bf16[64,128,128]{2,0,1:T(8,128)(2,1)S(1)}, u32[]{:S(2)}, u32[]{:S(2)}) async-start(bf16[64,128,128]{2,0,1:T(8,128)(2,1)} %bitcast.735), calls=%async_computation | async-start | bytes 4194304 | tf_op jit(solution)/shard_map/all_to_all | solution.py:16
  29.2 0.0 copy-done.1
  29.2 0.2 copy.834
  29.4 0.0 copy-done.2
  29.4 0.1 copy.841
  29.5 0.2 fusion.42
  29.8 0.2 fusion.41
  30.1 2.6 scatter_custom_fusion
  32.7 0.7 all_to_all.19
  33.4 0.0 copy-done.4
  33.4 49.8 %all-to-all-done = bf16[64,128,128]{2,0,1:T(8,128)(2,1)S(1)} async-done(((bf16[64,128,128]{2,0,1:T(8,128)(2,1)}), bf16[64,128,128]{2,0,1:T(8,128)(2,1)S(1)}, u32[]{:S(2)}, u32[]{:S(2)}) %all-to-all-start) | async-done | bytes 2097184 | tf_op jit(solution)/shard_map/all_to_all | solution.py:16
  83.2 6.1 %all-to-all-start.2 = ((s32[128,1,8]{2,1,0:T(1,128)}), s32[128,1,8]{2,1,0:T(1,128)S(1)}, u32[]{:S(2)}, u32[]{:S(2)}) async-start(s32[128,1,8]{2,1,0:T(1,128)} %bitcast.25), calls=%async_computation.2 | async-start | bytes 131072 | tf_op jit(solution)/shard_map/all_to_all | solution.py:75
  89.3 1.6 pad_maximum_fusion
  90.9 2.6 gather_fusion.1
  93.5 0.0 copy-start.3
  93.5 5.4 %fusion.10 = f32[64,135,128]{2,0,1:T(8,128)S(1)} fusion(bf16[1,135,128,128]{3,2,1,0:T(8,128)(2,1)} %param.12, bf16[135,64,128]{2,1,0:T(8,128)(2,1)S(1)} %gather_fusion.1), kind=kOutput, calls=%fused_computation.20 | convolution fusion | flops 283115520 | bytes 11059200 | tf_op jit(solution)/shard_map/ctj,tij->cti/dot_general | solution.py:19
  98.9 0.0 copy-done.3
  98.9 4.0 %fusion.34 = f32[64,8,128]{2,1,0:T(8,128)S(1)} fusion(f32[64,135,128]{2,0,1:T(8,128)S(1)} %fusion.10, s32[135]{0:T(256)S(1)} %bitcast.746), kind=kOutput, calls=%fused_computation.31 | convolution fusion | flops 106234936 | bytes 4686364 | tf_op jit(solution)/shard_map/rt,cti->cri/dot_general | solution.py:23
  102.9 0.2 copy.846
  103.1 0.1 fusion.40
  103.2 0.1 copy.838
  103.4 2.2 gather_fusion.2
  105.5 0.0 all-to-all-done.2
  105.5 13.7 %all-to-all-start.1 = ((bf16[64,128,128]{2,0,1:T(8,128)(2,1)}), bf16[64,128,128]{2,0,1:T(8,128)(2,1)S(1)}, u32[]{:S(2)}, u32[]{:S(2)}) async-start(bf16[64,128,128]{2,0,1:T(8,128)(2,1)} %bitcast.13), calls=%async_computation.1 | async-start | bytes 4194304 | tf_op jit(solution)/shard_map/all_to_all | solution.py:16
  119.3 0.1 reshape.198
  119.4 53.9 %all-to-all-done.1 = bf16[64,128,128]{2,0,1:T(8,128)(2,1)S(1)} async-done(((bf16[64,128,128]{2,0,1:T(8,128)(2,1)}), bf16[64,128,128]{2,0,1:T(8,128)(2,1)S(1)}, u32[]{:S(2)}, u32[]{:S(2)}) %all-to-all-start.1) | async-done | bytes 2097184 | tf_op jit(solution)/shard_map/all_to_all | solution.py:16
  173.3 1.6 pad_maximum_fusion.1
  174.9 2.6 gather_fusion.3
  177.5 5.4 %fusion.15 = f32[64,135,128]{2,0,1:T(8,128)S(1)} fusion(bf16[1,135,128,128]{3,2,1,0:T(8,128)(2,1)} %param.12, bf16[135,64,128]{2,1,0:T(8,128)(2,1)S(1)} %gather_fusion.3), kind=kOutput, calls=%fused_computation.21 | convolution fusion | flops 283115520 | bytes 11059200 | tf_op jit(solution)/shard_map/ctj,tij->cti/dot_general | solution.py:19
  182.9 4.0 %fusion.31 = f32[64,8,128]{2,1,0:T(8,128)S(1)} fusion(f32[64,135,128]{2,0,1:T(8,128)S(1)} %fusion.15, s32[135]{0:T(256)S(1)} %bitcast.747), kind=kOutput, calls=%fused_computation.30 | convolution fusion | flops 106234936 | bytes 4686364 | tf_op jit(solution)/shard_map/rt,cti->cri/dot_general | solution.py:23
  186.9 0.2 copy.850
  187.1 0.1 fusion.39
  187.2 3.2 %gather_fusion.5 = bf16[1024,64]{1,0:T(8,128)(2,1)S(1)} fusion(bf16[64,1024]{0,1:T(8,128)(2,1)S(1)} %fusion.39, s32[1024]{0:T(1024)S(1)} %broadcast_clamp_fusion), kind=kCustom, calls=%fused_computation.5 | custom fusion | bytes 266240 | tf_op jit(solution)/shard_map/gather | solution.py:74
  192.0 0.9 reshape.225
  192.9 6.2 %all-to-all-start.3 = ((bf16[128,2,256]{2,1,0:T(2,128)(2,1)}), bf16[128,2,256]{2,1,0:T(2,128)(2,1)S(1)}, u32[]{:S(2)}, u32[]{:S(2)}) async-start(bf16[128,2,256]{2,1,0:T(2,128)(2,1)} %reshape.225), calls=%async_computation.3 | async-start | bytes 262144 | tf_op jit(solution)/shard_map/all_to_all | solution.py:71
  199.0 0.3 all-reduce.2.cloned.1.call-start
  199.3 1.3 gather_fusion.4
  200.7 10.3 %all-to-all-done.3 = bf16[128,2,256]{2,1,0:T(2,128)(2,1)S(1)} async-done(((bf16[128,2,256]{2,1,0:T(2,128)(2,1)}), bf16[128,2,256]{2,1,0:T(2,128)(2,1)S(1)}, u32[]{:S(2)}, u32[]{:S(2)}) %all-to-all-start.3) | async-done | bytes 131104 | tf_op jit(solution)/shard_map/all_to_all | solution.py:71
  211.0 0.2 reshape.226
  211.2 0.0 copy-start.5
  211.2 0.0 copy-start.6
  211.3 3.1 %gather_fusion.6 = bf16[512,64]{1,0:T(8,128)(2,1)S(1)} fusion(bf16[64,128,8]{0,2,1:T(8,128)(2,1)S(1)} %bitcast_bitcast_fusion, s32[512]{0:T(512)S(1)} %bitcast.606), kind=kCustom, calls=%fused_computation.6 | custom fusion | bytes 135168 | tf_op jit(solution)/shard_map/gather | solution.py:87
  214.3 0.0 copy-done
  214.3 1.5 fusion.24
  215.8 0.0 all-reduce.2.cloned.1.call-update
  215.8 0.8 copy.845
  216.6 48.7 %all-reduce.2.cloned.1.call-done = bf16[1024,512]{0,1:T(8,128)(2,1)} async-done(((bf16[1024,512]{0,1:T(8,128)(2,1)}), bf16[1024,512]{0,1:T(8,128)(2,1)}) %all-reduce.2.cloned.1.call-update) | async-done | bytes 1048592 | tf_op jit(solution)/shard_map/psum | solution.py:93
  265.3 0.0 copy-done.5
  265.3 0.0 copy-done.6
  265.3 3.9 %fusion.20 = f32[1,512]{1,0:T(1,128)} fusion(f32[1024,1]{0,1:T(1,128)S(1)} %bitcast.750, bf16[1024,512]{0,1:T(8,128)(2,1)} %all-reduce.2.cloned.1.call-done, f32[1024]{0:T(1024)S(1)} %copy-done.6), kind=kOutput, calls=%fused_computation.22 | convolution fusion | flops 7864320 | bytes 1058816 | tf_op jit(solution)/shard_map/dot_general | solution.py:95
  (142 shorter events, 1.3 us)
Async XLA Ops:
  7.2 207.2 %copy-start = (bf16[64,1024]{1,0:T(8,128)(2,1)S(1)}, bf16[64,1024]{1,0:T(8,128)(2,1)}, u32[]{:S(2)}) copy-start(bf16[64,1024]{1,0:T(8,128)(2,1)} %param.19) | copy-start | bytes 393220
  11.7 17.5 %copy-start.1 = (bf16[64,1024]{1,0:T(8,128)(2,1)S(1)}, bf16[64,1024]{1,0:T(8,128)(2,1)}, u32[]{:S(2)}) copy-start(bf16[64,1024]{1,0:T(8,128)(2,1)} %param.11) | copy-start | bytes 393220
  11.7 17.7 %copy-start.2 = (s32[512,1]{0,1:T(1,128)S(1)}, s32[512,1]{0,1:T(1,128)}, u32[]{:S(2)}) copy-start(s32[512,1]{0,1:T(1,128)} %param.17) | copy-start | bytes 6148
  11.7 21.7 %copy-start.4 = (s32[1,135]{1,0:T(1,128)S(1)}, s32[1,135]{1,0:T(1,128)}, u32[]{:S(2)}) copy-start(s32[1,135]{1,0:T(1,128)} %param.14) | copy-start | bytes 1624
  11.7 71.6 %all-to-all-start = ((bf16[64,128,128]{2,0,1:T(8,128)(2,1)}), bf16[64,128,128]{2,0,1:T(8,128)(2,1)S(1)}, u32[]{:S(2)}, u32[]{:S(2)}) async-start(bf16[64,128,128]{2,0,1:T(8,128)(2,1)} %bitcast.735), calls=%async_computation | async-start | bytes 4194304 | tf_op jit(solution)/shard_map/all_to_all | solution.py:16
  83.2 22.3 %all-to-all-start.2 = ((s32[128,1,8]{2,1,0:T(1,128)}), s32[128,1,8]{2,1,0:T(1,128)S(1)}, u32[]{:S(2)}, u32[]{:S(2)}) async-start(s32[128,1,8]{2,1,0:T(1,128)} %bitcast.25), calls=%async_computation.2 | async-start | bytes 131072 | tf_op jit(solution)/shard_map/all_to_all | solution.py:75
  93.5 5.4 %copy-start.3 = (s32[1,135]{1,0:T(1,128)S(1)}, s32[1,135]{1,0:T(1,128)}, u32[]{:S(2)}) copy-start(s32[1,135]{1,0:T(1,128)} %param.13) | copy-start | bytes 1624
  105.5 67.8 %all-to-all-start.1 = ((bf16[64,128,128]{2,0,1:T(8,128)(2,1)}), bf16[64,128,128]{2,0,1:T(8,128)(2,1)S(1)}, u32[]{:S(2)}, u32[]{:S(2)}) async-start(bf16[64,128,128]{2,0,1:T(8,128)(2,1)} %bitcast.13), calls=%async_computation.1 | async-start | bytes 4194304 | tf_op jit(solution)/shard_map/all_to_all | solution.py:16
  192.9 18.1 %all-to-all-start.3 = ((bf16[128,2,256]{2,1,0:T(2,128)(2,1)}), bf16[128,2,256]{2,1,0:T(2,128)(2,1)S(1)}, u32[]{:S(2)}, u32[]{:S(2)}) async-start(bf16[128,2,256]{2,1,0:T(2,128)(2,1)} %reshape.225), calls=%async_computation.3 | async-start | bytes 262144 | tf_op jit(solution)/shard_map/all_to_all | solution.py:71
  199.0 66.3 %all-reduce.2.cloned.1.call-start = ((), (), s32[]{:S(2)}) async-start(), calls=%async_computation.4 | async-start | bytes 2097152 | tf_op jit(solution)/shard_map/psum | solution.py:93
  211.2 54.1 %copy-start.5 = (f32[1024]{0:T(1024)S(1)}, f32[1024]{0:T(1024)}, u32[]{:S(2)}) copy-start(f32[1024]{0:T(1024)} %param.21) | copy-start | bytes 12292
  211.2 54.1 %copy-start.6 = (f32[1024]{0:T(1024)S(1)}, f32[1024]{0:T(1024)}, u32[]{:S(2)}) copy-start(f32[1024]{0:T(1024)} %param.20) | copy-start | bytes 12292
Sparse Core Ops, SparseCore 0:
  215.9 49.3 all-reduce.1
